TPU v7x, 32 devices: a whole 2x2x4 slice. The times are simulated.
32 devices in a mesh: group: 8 (over y, x, core), tp: 4 (over z).
Axes of the slice: x: 2, y: 2, z: 4, core: 2. Of those that a mesh axis runs over, the one named last changes fastest.
Arguments:
- hidden: bfloat16 [2048, 8192], P('group', 'tp'), may hold values from -6 to 6
- w_kv: bfloat16 [8192, 2048], P('tp'), may hold values from -0.0625 to 0.0625
- prompt_lengths: int32 [2, 8], replicated, may hold values from 1 to 128, 256 in all within a row
- owner_step: int32 [2, 8], replicated, may hold values from 1 to 3
- cache: bfloat16 [64, 128, 2048], P(('group', 'tp')), may hold values from -8 to 8
- cache_len: int32 [64], P(('group', 'tp')), may hold values from 1 to 128
- queries: bfloat16 [64, 8192], P('group', 'tp'), may hold values from -200 to 200
- fresh: bfloat16 [64, 2048], P('group', 'tp'), may hold values from -10 to 10
- logits: bfloat16 [64, 30720], P('group', 'tp'), may hold values from -300 to 300
- states: int32 [64], P('group'), may hold values from 0 to 23
- masks: int32 [24, 1024], P(None, 'tp'), may hold values from 0 to 1073741823, as said below
Outputs:
- attended: bfloat16 [64, 8192], P('group', 'tp')
- logprob: float32 [64, 30720], P('group', 'tp')
Inputs may be any that keep to these rules, and one draw needn't show every extreme that they name: `prompt_lengths`: each row sums to 256; the longest prompt of every row has exactly 128 tokens. Prompt k of prefill group p goes to group p + owner_step[p, k] * 2. `masks`: every state allows at least one token in each aligned block of 7680 vocabulary entries.
All inputs are finite; a program needn't handle non-finite values.
Results may differ from a plain program's by a relative error of at most 0.02.
Values may be sent and summed in bfloat16 or wider, within the bound.
A program may use at most 64 MiB of HBM per device.

v0:
```python
import math
import jax
import jax.numpy as jnp
from jax import lax
from jax.sharding import PartitionSpec as P

HEADS = 64
KVH = 8
HD = 128
MAXLEN = 128
CACHE = 128
STATES = 24


def from_behind(block, axis, distance):
    devices = range(lax.axis_size(axis))
    route = [(i - distance, i) for i in devices if i - distance in devices]
    return lax.ppermute(block, axis, route)


def landing(slot_ids, source, turn_index, prompt_lengths, owner_step):
    chosen = owner_step[source] == turn_index
    ranking = jnp.cumsum(chosen.astype(jnp.int32)) - 1
    arrivals = jnp.sum(chosen.astype(jnp.int32))
    matched = chosen[None, :] & (ranking[None, :] == slot_ids[:, None])
    lengths = prompt_lengths[source]
    starts = jnp.cumsum(lengths) - lengths
    first_row = jnp.sum(jnp.where(matched, starts[None, :], 0), axis=1)
    prompt_len = jnp.sum(jnp.where(matched, lengths[None, :], 0), axis=1)
    landed = (slot_ids < arrivals) & (turn_index >= 1)
    return (landed, first_row, prompt_len)


def attend(query_rows, merged, alive_len, fresh_rows):
    row_count = merged.shape[0]
    group_size = HEADS // KVH
    key_rows = merged[:, :, : KVH * HD].reshape(row_count, CACHE, KVH, HD)
    value_rows = merged[:, :, KVH * HD :].reshape(row_count, CACHE, KVH, HD)
    queries = query_rows.reshape(row_count, KVH, group_size, HD)
    own_key = fresh_rows[:, : KVH * HD].reshape(row_count, KVH, HD)
    own_value = fresh_rows[:, KVH * HD :].reshape(row_count, KVH, HD)
    scaling = 1.0 / math.sqrt(HD)
    scores = (
        jnp.einsum("rkgd,rtkd->rkgt", queries, key_rows, preferred_element_type=jnp.float32)
        * scaling
    )
    own_score = (
        jnp.einsum("rkgd,rkd->rkg", queries, own_key, preferred_element_type=jnp.float32) * scaling
    )
    positions = jnp.arange(CACHE, dtype=jnp.int32)
    alive_mask = (positions[None, :] < alive_len[:, None])[:, None, None, :]
    highest = jnp.maximum(jnp.max(jnp.where(alive_mask, scores, -jnp.inf), axis=3), own_score)
    exponent = jnp.where(alive_mask, jnp.exp(scores - highest[..., None]), 0.0)
    own_exponent = jnp.exp(own_score - highest)
    denominator = jnp.sum(exponent, axis=3) + own_exponent
    weights = (exponent / denominator[..., None]).astype(jnp.bfloat16)
    own_weight = (own_exponent / denominator).astype(jnp.bfloat16)
    attended = jnp.einsum(
        "rkgt,rtkd->rkgd", weights, value_rows, preferred_element_type=jnp.float32
    )
    attended = (
        attended
        + own_weight.astype(jnp.float32)[..., None] * own_value.astype(jnp.float32)[:, :, None, :]
    )
    return attended.reshape(row_count, HEADS * HD).astype(jnp.bfloat16)


def per_device(
    hidden,
    w_kv,
    prompt_lengths,
    owner_step,
    cache,
    cache_len,
    queries,
    fresh,
    logits,
    states,
    masks,
):
    tensor_size = lax.axis_size("tp")
    groups = lax.axis_size("group")
    prefill = groups // 4
    group_index = lax.axis_index("group")
    column = lax.axis_index("tp")
    is_prefill = group_index < prefill
    source = group_index % prefill
    turn_index = group_index // prefill
    token_count = hidden.shape[0]
    kv_width = w_kv.shape[1]
    own_count = cache.shape[0]
    own_slots = jnp.arange(own_count, dtype=jnp.int32) * tensor_size + column
    landed, first_row, prompt_len = landing(
        own_slots, source, turn_index, prompt_lengths, owner_step
    )

    def compute():
        return jnp.dot(hidden, w_kv, preferred_element_type=jnp.float32)

    kv_piece = lax.psum_scatter(
        lax.cond(
            is_prefill,
            compute,
            lambda: jnp.zeros(
                (token_count // tensor_size * lax.axis_size("tp"), kv_width), jnp.float32
            ),
        ).astype(jnp.bfloat16),
        "tp",
        scatter_dimension=0,
        tiled=True,
    )
    arrived = [from_behind(kv_piece, "group", prefill * step_index) for step_index in (1, 2, 3)]
    incoming = jnp.where(
        turn_index == 1, arrived[0], jnp.where(turn_index == 2, arrived[1], arrived[2])
    )
    gathered = lax.all_gather(incoming, "tp", axis=0, tiled=True)
    padded = jnp.pad(gathered, ((0, MAXLEN), (0, 0)))
    handed = jax.vmap(lambda offset: lax.dynamic_slice_in_dim(padded, offset, MAXLEN, 0))(first_row)
    front = jnp.where(landed[:, None, None], handed, cache)
    merged = jnp.concatenate([front, cache[:, MAXLEN:]], axis=1)
    alive_len = jnp.where(landed, prompt_len, cache_len)
    mine_queries, mine_fresh = (
        lax.all_to_all(queries, "tp", split_axis=0, concat_axis=1, tiled=True),
        lax.all_to_all(fresh, "tp", split_axis=0, concat_axis=1, tiled=True),
    )
    attended = attend(mine_queries, merged, alive_len, mine_fresh)
    attended = lax.all_to_all(attended, "tp", split_axis=1, concat_axis=0, tiled=True)
    onehot = states[:, None] == jnp.arange(STATES, dtype=jnp.int32)[None, :]
    packed = jnp.sum(jnp.where(onehot[:, :, None], masks[None, :, :], 0), axis=1)
    shifts = jnp.arange(30, dtype=jnp.int32)
    bit_flags = jnp.bitwise_and(jnp.right_shift(packed[:, :, None], shifts[None, None, :]), 1)
    permitted = bit_flags.reshape(packed.shape[0], logits.shape[1]) == 1
    values = logits.astype(jnp.float32)
    local_peak = jnp.max(jnp.where(permitted, values, -jnp.inf), axis=1)
    highest = lax.pmax(local_peak, "tp")
    local_terms = jnp.sum(jnp.where(permitted, jnp.exp(values - highest[:, None]), 0.0), axis=1)
    denominator = lax.psum(local_terms, "tp")
    normalizer = highest + jnp.log(denominator)
    logprob = jnp.where(permitted, values - normalizer[:, None], 0.0)
    return (attended, logprob)


def solution(mesh):
    in_specs = (
        P("group", "tp"),
        P("tp", None),
        P(),
        P(),
        P(("group", "tp"), None, None),
        P(("group", "tp")),
        P("group", "tp"),
        P("group", "tp"),
        P("group", "tp"),
        P("group"),
        P(None, "tp"),
    )
    out_specs = (P("group", "tp"), P("group", "tp"))
    return jax.shard_map(
        per_device, mesh=mesh, in_specs=in_specs, out_specs=out_specs, check_vma=False
    )
```

profile of v0, /device:TPU:0, one launch (start us, length us, event | category | flops | bytes accessed | tf_op | source)
XLA Modules:
  0.0 112.0 jit_solution(17203343120737466503)
XLA Ops:
  7.2 0.0 reduce-scatter.2.cloned.1.call-start
  7.2 0.0 copy-start.5
  7.2 0.0 copy-start.9
  7.3 6.1 %conditional.1 = (bf16[256,2048]{1,0:T(8,128)(2,1)S(1)}) conditional(s32[]{:T(128)} %convert_element_type.47, () %tuple.14, (bf16[256,2048]{1,0:T(8,128)(2,1)}, bf16[2048,2048]{1,0:T(8,128)(2,1)}) %tuple.15), branch_computations={%region_3.4_spmd, %region_4.5_spmd} | conditional | flops 2147483648 | bytes 10485768 | solution.py:101
  7.3 6.1 %fusion.24 = bf16[256,2048]{1,0:T(8,128)(2,1)S(1)} fusion(bf16[256,2048]{1,0:T(8,128)(2,1)} %get-tuple-element.13, bf16[2048,2048]{1,0:T(8,128)(2,1)} %get-tuple-element.14), kind=kOutput, calls=%fused_computation.57 | convolution fusion | flops 2147483648 | bytes 10485760 | tf_op jit(solution)/shard_map/cond/branch_1_fun/dot_general | solution.py:98
  13.5 1.0 copy-done
  14.5 0.0 reduce-scatter.2.cloned.1.call-update
  14.5 0.0 copy-done.5
  14.5 0.6 all_to_all.41
  15.1 6.3 %all-to-all-start.1 = ((bf16[4,2,512]{2,1,0:T(2,128)(2,1)}), bf16[4,2,512]{2,1,0:T(2,128)(2,1)S(1)}, u32[]{:S(2)}, u32[]{:S(2)}) async-start(bf16[4,2,512]{2,1,0:T(2,128)(2,1)} %all_to_all.41), calls=%async_computation.2 | async-start | bytes 16384 | tf_op jit(solution)/shard_map/all_to_all | solution.py:124
  21.5 0.0 copy-done.9
  21.5 0.1 iota_compare_fusion
  21.5 0.1 select_reduce_fusion
  21.6 0.3 shift_right_arithmetic.20
  22.0 0.5 shift_right_arithmetic.21
  22.5 0.1 shift_right_arithmetic.23
  22.6 0.0 copy-done.1
  22.6 0.2 fusion.1
  22.8 12.6 %pmax.7 = f32[8]{0:T(128)S(1)} all-reduce(f32[8]{0:T(128)S(1)} %get-tuple-element.49), channel_id=1, replica_groups=mesh['group'=8,'tp'=4] {'tp'}, use_global_device_ids=true, to_apply=%region_12.13 | all-reduce | flops 8 | bytes 64 | tf_op jit(solution)/shard_map/pmax | solution.py:135
  35.5 0.2 reduce-window_1_clone.1
  35.7 0.3 fusion.4
  35.9 7.2 %reduce-scatter.2.cloned.1.call-done = bf16[64,2048]{1,0:T(8,128)(2,1)} async-done(((bf16[256,2048]{1,0:T(8,128)(2,1)}), bf16[64,2048]{1,0:T(8,128)(2,1)}) %reduce-scatter.2.cloned.1.call-update) | async-done | bytes 262160 | tf_op jit(solution)/shard_map/reduce_scatter | solution.py:100
  43.1 3.1 %collective-permute-start = (bf16[64,2048]{1,0:T(8,128)(2,1)}, bf16[64,2048]{1,0:T(8,128)(2,1)S(1)}, u32[]{:S(2)}, u32[]{:S(2)}) collective-permute-start(bf16[64,2048]{1,0:T(8,128)(2,1)} %reduce-scatter.2.cloned.1.call-done), channel_id=1, source_target_pairs={{0,8},{4,12},{8,16},{12,20},{16,24},{20,28},{1,9},{5,13},{9,17},{1... | collective-permute-start | bytes 786440 | tf_op jit(solution)/shard_map/ppermute | solution.py:18
  46.2 3.4 %collective-permute-start.1 = (bf16[64,2048]{1,0:T(8,128)(2,1)}, bf16[64,2048]{1,0:T(8,128)(2,1)S(1)}, u32[]{:S(2)}, u32[]{:S(2)}) collective-permute-start(bf16[64,2048]{1,0:T(8,128)(2,1)} %reduce-scatter.2.cloned.1.call-done), channel_id=1, source_target_pairs={{0,16},{4,20},{8,24},{12,28},{1,17},{5,21},{9,25},{13,29},{2,18},{... | collective-permute-start | bytes 786440 | tf_op jit(solution)/shard_map/ppermute | solution.py:18
  49.6 1.3 %collective-permute-start.2 = (bf16[64,2048]{1,0:T(8,128)(2,1)}, bf16[64,2048]{1,0:T(8,128)(2,1)S(1)}, u32[]{:S(2)}, u32[]{:S(2)}) collective-permute-start(bf16[64,2048]{1,0:T(8,128)(2,1)} %reduce-scatter.2.cloned.1.call-done), channel_id=1, source_target_pairs={{0,24},{4,28},{1,25},{5,29},{2,26},{6,30},{3,27},{7,31}} | collective-permute-start | bytes 786440 | tf_op jit(solution)/shard_map/ppermute | solution.py:18
  50.9 0.0 copy-done.6
  51.0 0.2 reduce-window.9
  51.2 1.7 %collective-permute-done = bf16[64,2048]{1,0:T(8,128)(2,1)S(1)} collective-permute-done((bf16[64,2048]{1,0:T(8,128)(2,1)}, bf16[64,2048]{1,0:T(8,128)(2,1)S(1)}, u32[]{:S(2)}, u32[]{:S(2)}) %collective-permute-start) | collective-permute-done | bytes 262176 | tf_op jit(solution)/shard_map/ppermute | solution.py:18
  52.9 5.3 %collective-permute-done.1 = bf16[64,2048]{1,0:T(8,128)(2,1)S(1)} collective-permute-done((bf16[64,2048]{1,0:T(8,128)(2,1)}, bf16[64,2048]{1,0:T(8,128)(2,1)S(1)}, u32[]{:S(2)}, u32[]{:S(2)}) %collective-permute-start.1) | collective-permute-done | bytes 262176 | tf_op jit(solution)/shard_map/ppermute | solution.py:18
  58.2 0.0 collective-permute-done.2
  58.2 0.8 select_select_fusion
  59.0 0.0 all-gather.2.cloned.1.call-update
  59.0 9.2 %psum.7 = f32[8]{0:T(128)S(1)} all-reduce(f32[8]{0:T(128)S(1)} %fusion.4), channel_id=1, replica_groups=mesh['group'=8,'tp'=4] {'tp'}, use_global_device_ids=true, to_apply=%region_14.15 | all-reduce | flops 8 | bytes 64 | tf_op jit(solution)/shard_map/psum | solution.py:137
  68.2 0.6 fusion.19
  68.8 0.2 fusion.16
  69.0 0.0 copy-done.7
  69.0 0.7 fusion.21
  69.7 0.1 iota_compare_fusion.1
  69.8 0.1 copy.46
  69.9 1.3 %copy.34 = bf16[2,128,2048]{1,2,0:T(8,128)(2,1)} copy(bf16[2,128,2048]{2,1,0:T(8,128)(2,1)S(1)} %copy-done.2) | data formatting | bytes 2097152 | tf_op args[4]
  71.2 0.6 all_to_all.38
  71.8 0.0 all-to-all-done.1
  71.8 3.3 %all-to-all-start = ((bf16[4,2,2048]{2,1,0:T(2,128)(2,1)}), bf16[4,2,2048]{2,1,0:T(2,128)(2,1)S(1)}, u32[]{:S(2)}, u32[]{:S(2)}) async-start(bf16[4,2,2048]{2,1,0:T(2,128)(2,1)} %all_to_all.38), calls=%async_computation.1 | async-start | bytes 65536 | tf_op jit(solution)/shard_map/all_to_all | solution.py:123
  75.2 6.0 %all-to-all-done = bf16[4,2,2048]{2,1,0:T(2,128)(2,1)S(1)} async-done(((bf16[4,2,2048]{2,1,0:T(2,128)(2,1)}), bf16[4,2,2048]{2,1,0:T(2,128)(2,1)S(1)}, u32[]{:S(2)}, u32[]{:S(2)}) %all-to-all-start) | async-done | bytes 32800 | tf_op jit(solution)/shard_map/all_to_all | solution.py:123
  81.2 0.1 fusion.25
  81.3 6.8 %all-gather.2.cloned.1.call-done = bf16[256,2048]{1,0:T(8,128)(2,1)} async-done(((bf16[64,2048]{1,0:T(8,128)(2,1)}), bf16[256,2048]{1,0:T(8,128)(2,1)}) %all-gather.2.cloned.1.call-update) | async-done | bytes 1048592 | tf_op jit(solution)/shard_map/all_gather | solution.py:116
  88.2 1.4 %pad.5 = bf16[384,2048]{1,0:T(8,128)(2,1)S(1)} pad(bf16[256,2048]{1,0:T(8,128)(2,1)} %all-gather.2.cloned.1.call-done, bf16[]{:T(256)} %constant.55.clone.1), padding=0_128x0_0 | pad | bytes 2621442 | tf_op jit(solution)/shard_map/jit(_pad)/pad | solution.py:117
  89.6 2.7 %while.1 = (s32[]{:T(128)}, bf16[384,2048]{1,0:T(8,128)(2,1)S(1)}, s32[2,2]{1,0:T(2,128)S(1)}, bf16[2,128,2048]{1,2,0:T(8,128)(2,1)}, s32[]{:T(128)}) while((s32[]{:T(128)}, bf16[384,2048]{1,0:T(8,128)(2,1)S(1)}, s32[2,2]{1,0:T(2,128)S(1)}, bf16[2,128,2048]{1,2,0:T(8,128)(2,1)}, s32[]{:T(128)}) %tuple.40), condition=%wide.while_cond, body=%wide.while_body.sunk | while | flops 2 | bytes 3146325 | solution.py:118
  89.6 0.2 dynamic-slice_bitcast_fusion.2
  89.8 0.3 copy.51
  90.0 0.9 constant_dynamic-update-slice_fusion.2
  90.9 0.2 dynamic-slice_bitcast_fusion.2
  91.1 0.3 copy.51
  91.4 0.9 constant_dynamic-update-slice_fusion.2
  92.2 1.7 %broadcast_select_fusion = bf16[2,128,2048]{1,2,0:T(8,128)(2,1)S(1)} fusion(bf16[2,128,2048]{1,2,0:T(8,128)(2,1)} %get-tuple-element.22, bf16[2,128,2048]{1,2,0:T(8,128)(2,1)} %copy.34, pred[2]{0:T(512)(128)(4,1)S(1)} %get-tuple-element.52), kind=kLoop, calls=%fused_computation.6 | loop fusion | flops 524288 | bytes 3145730 | tf_op jit(solution)/shard_map/jit(_where)/select_n | solution.py:119
  93.9 0.1 fusion.22
  94.0 0.3 select_reduce_fusion.1
  94.3 0.2 bitcast_reduce_fusion
  94.5 0.4 fusion
  95.0 0.7 copy.38
  95.6 3.3 %all-to-all-start.2 = ((bf16[2,4,2048]{2,0,1:T(2,128)(2,1)}), bf16[2,4,2048]{2,0,1:T(2,128)(2,1)S(1)}, u32[]{:S(2)}, u32[]{:S(2)}) async-start(bf16[2,4,2048]{2,0,1:T(2,128)(2,1)} %copy.38), calls=%async_computation.3 | async-start | bytes 65536 | tf_op jit(solution)/shard_map/all_to_all | solution.py:127
  98.9 0.8 fusion.5
  99.7 4.8 %all-to-all-done.2 = bf16[2,4,2048]{2,0,1:T(2,128)(2,1)S(1)} async-done(((bf16[2,4,2048]{2,0,1:T(2,128)(2,1)}), bf16[2,4,2048]{2,0,1:T(2,128)(2,1)S(1)}, u32[]{:S(2)}, u32[]{:S(2)}) %all-to-all-start.2) | async-done | bytes 32800 | tf_op jit(solution)/shard_map/all_to_all | solution.py:127
  104.5 0.6 all_to_all.47
  (34 shorter events, 0.2 us)
Async XLA Ops:
  7.2 35.9 %reduce-scatter.2.cloned.1.call-start = ((), (), s32[]{:S(2)}) async-start(), calls=%async_computation.4 | async-start | bytes 1310720 | tf_op jit(solution)/shard_map/reduce_scatter | solution.py:100
  7.2 7.3 %copy-start.5 = (bf16[8,512]{1,0:T(8,128)(2,1)S(1)}, bf16[8,512]{1,0:T(8,128)(2,1)}, u32[]{:S(2)}) copy-start(bf16[8,512]{1,0:T(8,128)(2,1)} %param.20) | copy-start | bytes 24580
  7.2 14.2 %copy-start.9 = (s32[8]{0:T(128)S(1)}, s32[8]{0:T(128)}, u32[]{:S(2)}) copy-start(s32[8]{0:T(128)} %param.22) | copy-start | bytes 100
  7.2 14.3 %copy-start.4 = (s32[24,256]{1,0:T(8,128)S(1)}, s32[24,256]{1,0:T(8,128)}, u32[]{:S(2)}) copy-start(s32[24,256]{1,0:T(8,128)} %param.23) | copy-start | bytes 73732
  7.3 15.4 %copy-start.1 = (bf16[8,7680]{1,0:T(8,128)(2,1)S(1)}, bf16[8,7680]{1,0:T(8,128)(2,1)}, u32[]{:S(2)}) copy-start(bf16[8,7680]{1,0:T(8,128)(2,1)} %param.21) | copy-start | bytes 368644
  7.3 28.2 %copy-start.8 = (s32[2,8]{1,0:T(2,128)S(1)}, s32[2,8]{1,0:T(2,128)}, u32[]{:S(2)}) copy-start(s32[2,8]{1,0:T(2,128)} %param.15) | copy-start | bytes 196
  7.3 43.7 %copy-start.6 = (s32[2,8]{1,0:T(2,128)S(1)}, s32[2,8]{1,0:T(2,128)}, u32[]{:S(2)}) copy-start(s32[2,8]{1,0:T(2,128)} %param.16) | copy-start | bytes 196
  7.3 61.7 %copy-start.7 = (s32[2]{0:T(128)S(1)}, s32[2]{0:T(128)}, u32[]{:S(2)}) copy-start(s32[2]{0:T(128)} %param.18) | copy-start | bytes 28
  7.3 62.6 %copy-start.2 = (bf16[2,128,2048]{2,1,0:T(8,128)(2,1)S(1)}, bf16[2,128,2048]{2,1,0:T(8,128)(2,1)}, u32[]{:S(2)}) copy-start(bf16[2,128,2048]{2,1,0:T(8,128)(2,1)} %param.17) | copy-start | bytes 3145732
  7.3 63.9 %copy-start.3 = (bf16[8,2048]{1,0:T(8,128)(2,1)S(1)}, bf16[8,2048]{1,0:T(8,128)(2,1)}, u32[]{:S(2)}) copy-start(bf16[8,2048]{1,0:T(8,128)(2,1)} %param.19) | copy-start | bytes 98308
  13.5 1.0 copy-start
  15.1 56.7 %all-to-all-start.1 = ((bf16[4,2,512]{2,1,0:T(2,128)(2,1)}), bf16[4,2,512]{2,1,0:T(2,128)(2,1)S(1)}, u32[]{:S(2)}, u32[]{:S(2)}) async-start(bf16[4,2,512]{2,1,0:T(2,128)(2,1)} %all_to_all.41), calls=%async_computation.2 | async-start | bytes 16384 | tf_op jit(solution)/shard_map/all_to_all | solution.py:124
  21.5 66.7 %all-gather.2.cloned.1.call-start = ((), (), s32[]{:S(2)}) async-start(), calls=%async_computation.5 | async-start | bytes 1310720 | tf_op jit(solution)/shard_map/all_gather | solution.py:116
  43.1 9.8 %collective-permute-start = (bf16[64,2048]{1,0:T(8,128)(2,1)}, bf16[64,2048]{1,0:T(8,128)(2,1)S(1)}, u32[]{:S(2)}, u32[]{:S(2)}) collective-permute-start(bf16[64,2048]{1,0:T(8,128)(2,1)} %reduce-scatter.2.cloned.1.call-done), channel_id=1, source_target_pairs={{0,8},{4,12},{8,16},{12,20},{16,24},{20,28},{1,9},{5,13},{9,17},{1... | collective-permute-start | bytes 786440 | tf_op jit(solution)/shard_map/ppermute | solution.py:18
  46.2 12.0 %collective-permute-start.1 = (bf16[64,2048]{1,0:T(8,128)(2,1)}, bf16[64,2048]{1,0:T(8,128)(2,1)S(1)}, u32[]{:S(2)}, u32[]{:S(2)}) collective-permute-start(bf16[64,2048]{1,0:T(8,128)(2,1)} %reduce-scatter.2.cloned.1.call-done), channel_id=1, source_target_pairs={{0,16},{4,20},{8,24},{12,28},{1,17},{5,21},{9,25},{13,29},{2,18},{... | collective-permute-start | bytes 786440 | tf_op jit(solution)/shard_map/ppermute | solution.py:18
  49.6 8.6 %collective-permute-start.2 = (bf16[64,2048]{1,0:T(8,128)(2,1)}, bf16[64,2048]{1,0:T(8,128)(2,1)S(1)}, u32[]{:S(2)}, u32[]{:S(2)}) collective-permute-start(bf16[64,2048]{1,0:T(8,128)(2,1)} %reduce-scatter.2.cloned.1.call-done), channel_id=1, source_target_pairs={{0,24},{4,28},{1,25},{5,29},{2,26},{6,30},{3,27},{7,31}} | collective-permute-start | bytes 786440 | tf_op jit(solution)/shard_map/ppermute | solution.py:18
  71.8 9.3 %all-to-all-start = ((bf16[4,2,2048]{2,1,0:T(2,128)(2,1)}), bf16[4,2,2048]{2,1,0:T(2,128)(2,1)S(1)}, u32[]{:S(2)}, u32[]{:S(2)}) async-start(bf16[4,2,2048]{2,1,0:T(2,128)(2,1)} %all_to_all.38), calls=%async_computation.1 | async-start | bytes 65536 | tf_op jit(solution)/shard_map/all_to_all | solution.py:123
  95.6 8.9 %all-to-all-start.2 = ((bf16[2,4,2048]{2,0,1:T(2,128)(2,1)}), bf16[2,4,2048]{2,0,1:T(2,128)(2,1)S(1)}, u32[]{:S(2)}, u32[]{:S(2)}) async-start(bf16[2,4,2048]{2,0,1:T(2,128)(2,1)} %copy.38), calls=%async_computation.3 | async-start | bytes 65536 | tf_op jit(solution)/shard_map/all_to_all | solution.py:127
Sparse Core Ops, SparseCore 0:
  14.6 28.4 reduce-scatter.1
  59.1 28.9 all-gather.1
where the time goes:
time: 113 us; the launch traced here: 112 us
  waiting for transfers between devices  31.9 us (28%)
  blocking collectives  21.8 us (19%)
  starting transfers between devices  20.7 us (18%)
  between operations  14.3 us (13%)
  local copies, waits for them, and re-layouts  10.1 us (9%)
  matrix products  7 us (6%)
  other arithmetic  6.08 us (5%)
    pmax x1, blocking collectives, per_device(): highest = lax.pmax(local_peak, 'tp')  12.6 us
    psum x1, blocking collectives, per_device(): denominator = lax.psum(local_terms, 'tp')  9.17 us
    ppermute x3, starting transfers between devices, from_behind(): return lax.ppermute(block, axis, route)  7.82 us
    reduce_scatter x1, waiting for transfers between devices, per_device(): lax.psum_scatter(lax.cond(is_prefill, compute, lambda: jnp.zeros((token_c...  7.16 us
    ppermute x3, waiting for transfers between devices, from_behind(): return lax.ppermute(block, axis, route)  7.05 us
    all_gather x1, waiting for transfers between devices, per_device(): gathered = lax.all_gather(incoming, 'tp', axis=0, tiled=True)  6.82 us
    all_to_all x1, starting transfers between devices, per_device(): lax.all_to_all(fresh, 'tp', split_axis=0, concat_axis=1, tiled=True)  6.35 us
    dot_general x1, matrix products, compute(): return jnp.dot(hidden, w_kv, preferred_element_type=jnp.float32)  6.13 us
  transfers between devices with their start and end apart: 8, of which 6 were waited for; matrix products, arithmetic and copies ran while one was open for 6% of the time, Pallas kernels for 0%

commit v1 on v0

--- a/solution.py
+++ b/solution.py
@@ -134,7 +134,11 @@
     local_peak = jnp.max(jnp.where(permitted, values, -jnp.inf), axis=1)
     highest = lax.pmax(local_peak, "tp")
     local_terms = jnp.sum(jnp.where(permitted, jnp.exp(values - highest[:, None]), 0.0), axis=1)
-    denominator = lax.psum(local_terms, "tp")
+    denominator = local_terms
+    for hop in (1, 2):
+        denominator = denominator + lax.ppermute(
+            denominator, "tp", [(dev, dev ^ hop) for dev in range(4)]
+        )
     normalizer = highest + jnp.log(denominator)
     logprob = jnp.where(permitted, values - normalizer[:, None], 0.0)
     return (attended, logprob)

time: 113 us -> 112 us (level)
  blocking collectives: 21.8 us -> 12.6 us
  waiting for transfers between devices: 31.9 us -> 39.7 us
  starting transfers between devices: 20.7 us -> 22.2 us
    psum x1 -> x0, blocking collectives: 9.17 us -> none  [per_device(): denominator = lax.psum(local_terms, 'tp')]
    all_gather x1, waiting for transfers between devices: 6.82 us -> 11.6 us  [per_device(): gathered = lax.all_gather(incoming, 'tp', axis=0, tiled=True)]
    ppermute x0 -> x2, waiting for transfers between devices: none -> 3.2 us  [per_device(): lax.ppermute(denominator, 'tp', [(dev, dev ^ hop) for dev in range(4)])]
    ppermute x0 -> x2, starting transfers between devices: none -> 1.39 us  [per_device(): lax.ppermute(denominator, 'tp', [(dev, dev ^ hop) for dev in range(4)])]
  transfers between devices with their start and end apart: 8 -> 10, of which waited for: 6 -> 7; matrix products, arithmetic and copies ran while one was open for 6% -> 6% of each run, Pallas kernels for 0% -> 0%
where the time goes in v1:
time: 112 us
  waiting for transfers between devices  39.7 us (35%)
  starting transfers between devices  22.2 us (20%)
  between operations  14.4 us (13%)
  blocking collectives  12.6 us (11%)
  local copies, waits for them, and re-layouts  10 us (9%)
  matrix products  7 us (6%)
  other arithmetic  5.98 us (5%)
    pmax x1, blocking collectives, per_device(): highest = lax.pmax(local_peak, 'tp')  12.6 us
    all_gather x1, waiting for transfers between devices, per_device(): gathered = lax.all_gather(incoming, 'tp', axis=0, tiled=True)  11.6 us
    ppermute x3, starting transfers between devices, from_behind(): return lax.ppermute(block, axis, route)  7.83 us
    reduce_scatter x1, waiting for transfers between devices, per_device(): lax.psum_scatter(lax.cond(is_prefill, compute, lambda: jnp.zeros((token_c...  7.04 us
    ppermute x3, waiting for transfers between devices, from_behind(): return lax.ppermute(block, axis, route)  7.01 us
    all_to_all x1, starting transfers between devices, per_device(): lax.all_to_all(fresh, 'tp', split_axis=0, concat_axis=1, tiled=True)  6.35 us
    dot_general x1, matrix products, compute(): return jnp.dot(hidden, w_kv, preferred_element_type=jnp.float32)  6.13 us
    all_to_all x1, waiting for transfers between devices, per_device(): lax.all_to_all(queries, 'tp', split_axis=0, concat_axis=1, tiled=True)  5.96 us
  transfers between devices with their start and end apart: 10, of which 7 were waited for; matrix products, arithmetic and copies ran while one was open for 6% of the time, Pallas kernels for 0%

profile of v1, /device:TPU:0, one launch (start us, length us, event | category | flops | bytes accessed | tf_op | source)
XLA Modules:
  0.0 112.0 jit_solution(4605166776224155049)
XLA Ops:
  7.2 0.0 reduce-scatter.2.cloned.1.call-start
  7.2 0.0 copy-start.5
  7.2 0.0 copy-start.9
  7.2 0.0 copy-start.4
  7.3 6.1 %conditional.1 = (bf16[256,2048]{1,0:T(8,128)(2,1)S(1)}) conditional(s32[]{:T(128)} %convert_element_type.47, () %tuple.14, (bf16[256,2048]{1,0:T(8,128)(2,1)}, bf16[2048,2048]{1,0:T(8,128)(2,1)}) %tuple.15), branch_computations={%region_3.4_spmd, %region_4.5_spmd} | conditional | flops 2147483648 | bytes 10485768 | solution.py:101
  7.3 6.1 %fusion.24 = bf16[256,2048]{1,0:T(8,128)(2,1)S(1)} fusion(bf16[256,2048]{1,0:T(8,128)(2,1)} %get-tuple-element.13, bf16[2048,2048]{1,0:T(8,128)(2,1)} %get-tuple-element.14), kind=kOutput, calls=%fused_computation.57 | convolution fusion | flops 2147483648 | bytes 10485760 | tf_op jit(solution)/shard_map/cond/branch_1_fun/dot_general | solution.py:98
  13.5 1.0 copy-done
  14.4 0.0 reduce-scatter.2.cloned.1.call-update
  14.5 0.6 all_to_all.41
  15.1 6.3 %all-to-all-start.1 = ((bf16[4,2,512]{2,1,0:T(2,128)(2,1)}), bf16[4,2,512]{2,1,0:T(2,128)(2,1)S(1)}, u32[]{:S(2)}, u32[]{:S(2)}) async-start(bf16[4,2,512]{2,1,0:T(2,128)(2,1)} %all_to_all.41), calls=%async_computation.2 | async-start | bytes 16384 | tf_op jit(solution)/shard_map/all_to_all | solution.py:124
  21.4 0.0 copy-done.9
  21.4 0.1 iota_compare_fusion
  21.5 0.1 select_reduce_fusion
  21.6 0.3 shift_right_arithmetic.20
  22.0 0.5 shift_right_arithmetic.21
  22.5 0.1 shift_right_arithmetic.23
  22.6 0.2 fusion.1
  22.8 12.6 %pmax.7 = f32[8]{0:T(128)S(1)} all-reduce(f32[8]{0:T(128)S(1)} %get-tuple-element.49), channel_id=1, replica_groups=mesh['group'=8,'tp'=4] {'tp'}, use_global_device_ids=true, to_apply=%region_12.13 | all-reduce | flops 8 | bytes 64 | tf_op jit(solution)/shard_map/pmax | solution.py:135
  35.4 0.3 fusion.4
  35.7 0.1 collective-permute-start.3
  35.8 0.2 reduce-window_1_clone.1
  36.0 7.0 %reduce-scatter.2.cloned.1.call-done = bf16[64,2048]{1,0:T(8,128)(2,1)} async-done(((bf16[256,2048]{1,0:T(8,128)(2,1)}), bf16[64,2048]{1,0:T(8,128)(2,1)}) %reduce-scatter.2.cloned.1.call-update) | async-done | bytes 262160 | tf_op jit(solution)/shard_map/reduce_scatter | solution.py:100
  43.1 3.1 %collective-permute-start = (bf16[64,2048]{1,0:T(8,128)(2,1)}, bf16[64,2048]{1,0:T(8,128)(2,1)S(1)}, u32[]{:S(2)}, u32[]{:S(2)}) collective-permute-start(bf16[64,2048]{1,0:T(8,128)(2,1)} %reduce-scatter.2.cloned.1.call-done), channel_id=1, source_target_pairs={{0,8},{4,12},{8,16},{12,20},{16,24},{20,28},{1,9},{5,13},{9,17},{1... | collective-permute-start | bytes 786440 | tf_op jit(solution)/shard_map/ppermute | solution.py:18
  46.2 3.4 %collective-permute-start.1 = (bf16[64,2048]{1,0:T(8,128)(2,1)}, bf16[64,2048]{1,0:T(8,128)(2,1)S(1)}, u32[]{:S(2)}, u32[]{:S(2)}) collective-permute-start(bf16[64,2048]{1,0:T(8,128)(2,1)} %reduce-scatter.2.cloned.1.call-done), channel_id=1, source_target_pairs={{0,16},{4,20},{8,24},{12,28},{1,17},{5,21},{9,25},{13,29},{2,18},{... | collective-permute-start | bytes 786440 | tf_op jit(solution)/shard_map/ppermute | solution.py:18
  49.6 1.3 %collective-permute-start.2 = (bf16[64,2048]{1,0:T(8,128)(2,1)}, bf16[64,2048]{1,0:T(8,128)(2,1)S(1)}, u32[]{:S(2)}, u32[]{:S(2)}) collective-permute-start(bf16[64,2048]{1,0:T(8,128)(2,1)} %reduce-scatter.2.cloned.1.call-done), channel_id=1, source_target_pairs={{0,24},{4,28},{1,25},{5,29},{2,26},{6,30},{3,27},{7,31}} | collective-permute-start | bytes 786440 | tf_op jit(solution)/shard_map/ppermute | solution.py:18
  51.0 0.2 reduce-window.9
  51.2 1.7 %collective-permute-done = bf16[64,2048]{1,0:T(8,128)(2,1)S(1)} collective-permute-done((bf16[64,2048]{1,0:T(8,128)(2,1)}, bf16[64,2048]{1,0:T(8,128)(2,1)S(1)}, u32[]{:S(2)}, u32[]{:S(2)}) %collective-permute-start) | collective-permute-done | bytes 262176 | tf_op jit(solution)/shard_map/ppermute | solution.py:18
  52.9 5.3 %collective-permute-done.1 = bf16[64,2048]{1,0:T(8,128)(2,1)S(1)} collective-permute-done((bf16[64,2048]{1,0:T(8,128)(2,1)}, bf16[64,2048]{1,0:T(8,128)(2,1)S(1)}, u32[]{:S(2)}, u32[]{:S(2)}) %collective-permute-start.1) | collective-permute-done | bytes 262176 | tf_op jit(solution)/shard_map/ppermute | solution.py:18
  58.2 0.0 collective-permute-done.2
  58.2 0.7 select_select_fusion
  58.9 0.0 all-gather.2.cloned.1.call-update
  59.0 0.2 fusion.16
  59.2 0.1 copy.46
  59.3 1.3 %copy.34 = bf16[2,128,2048]{1,2,0:T(8,128)(2,1)} copy(bf16[2,128,2048]{2,1,0:T(8,128)(2,1)S(1)} %copy-done.2) | data formatting | bytes 2097152 | tf_op args[4]
  60.6 0.6 all_to_all.38
  61.2 0.6 fusion.19
  61.9 0.6 fusion.21
  62.4 0.1 iota_compare_fusion.1
  62.5 0.0 collective-permute-done.3
  62.5 1.3 %collective-permute-start.4 = (f32[8]{0:T(128)S(1)}, f32[8]{0:T(128)S(1)}, u32[]{:S(2)}, u32[]{:S(2)}) collective-permute-start(f32[8]{0:T(128)S(1)} %add.67), channel_id=1, source_target_pairs={{0,2},{1,3},{2,0},{3,1},{4,6},{5,7},{6,4},{7,5},{8,10},{9,11},{10,... | collective-permute-start | bytes 104 | tf_op jit(solution)/shard_map/ppermute | solution.py:139
  63.9 3.2 %collective-permute-done.4 = f32[8]{0:T(128)S(1)} collective-permute-done((f32[8]{0:T(128)S(1)}, f32[8]{0:T(128)S(1)}, u32[]{:S(2)}, u32[]{:S(2)}) %collective-permute-start.4) | collective-permute-done | bytes 64 | tf_op jit(solution)/shard_map/ppermute | solution.py:139
  67.1 0.0 all-to-all-done.1
  67.1 3.3 %all-to-all-start = ((bf16[4,2,2048]{2,1,0:T(2,128)(2,1)}), bf16[4,2,2048]{2,1,0:T(2,128)(2,1)S(1)}, u32[]{:S(2)}, u32[]{:S(2)}) async-start(bf16[4,2,2048]{2,1,0:T(2,128)(2,1)} %all_to_all.38), calls=%async_computation.1 | async-start | bytes 65536 | tf_op jit(solution)/shard_map/all_to_all | solution.py:123
  70.4 6.0 %all-to-all-done = bf16[4,2,2048]{2,1,0:T(2,128)(2,1)S(1)} async-done(((bf16[4,2,2048]{2,1,0:T(2,128)(2,1)}), bf16[4,2,2048]{2,1,0:T(2,128)(2,1)S(1)}, u32[]{:S(2)}, u32[]{:S(2)}) %all-to-all-start) | async-done | bytes 32800 | tf_op jit(solution)/shard_map/all_to_all | solution.py:123
  76.4 0.1 fusion.25
  76.5 11.6 %all-gather.2.cloned.1.call-done = bf16[256,2048]{1,0:T(8,128)(2,1)} async-done(((bf16[64,2048]{1,0:T(8,128)(2,1)}), bf16[256,2048]{1,0:T(8,128)(2,1)}) %all-gather.2.cloned.1.call-update) | async-done | bytes 1048592 | tf_op jit(solution)/shard_map/all_gather | solution.py:116
  88.1 1.4 %pad.5 = bf16[384,2048]{1,0:T(8,128)(2,1)S(1)} pad(bf16[256,2048]{1,0:T(8,128)(2,1)} %all-gather.2.cloned.1.call-done, bf16[]{:T(256)} %constant.55.clone.1), padding=0_128x0_0 | pad | bytes 2621442 | tf_op jit(solution)/shard_map/jit(_pad)/pad | solution.py:117
  89.5 2.6 %while.1 = (s32[]{:T(128)}, bf16[384,2048]{1,0:T(8,128)(2,1)S(1)}, s32[2,2]{1,0:T(2,128)S(1)}, bf16[2,128,2048]{1,2,0:T(8,128)(2,1)}, s32[]{:T(128)}) while((s32[]{:T(128)}, bf16[384,2048]{1,0:T(8,128)(2,1)S(1)}, s32[2,2]{1,0:T(2,128)S(1)}, bf16[2,128,2048]{1,2,0:T(8,128)(2,1)}, s32[]{:T(128)}) %tuple.40), condition=%wide.while_cond, body=%wide.while_body.sunk | while | flops 2 | bytes 3146325 | solution.py:118
  89.6 0.2 dynamic-slice_bitcast_fusion.2
  89.7 0.3 copy.51
  90.0 0.8 constant_dynamic-update-slice_fusion.2
  90.9 0.2 dynamic-slice_bitcast_fusion.2
  91.0 0.3 copy.51
  91.3 0.8 constant_dynamic-update-slice_fusion.2
  92.2 1.7 %broadcast_select_fusion = bf16[2,128,2048]{1,2,0:T(8,128)(2,1)S(1)} fusion(bf16[2,128,2048]{1,2,0:T(8,128)(2,1)} %get-tuple-element.22, bf16[2,128,2048]{1,2,0:T(8,128)(2,1)} %copy.34, pred[2]{0:T(512)(128)(4,1)S(1)} %get-tuple-element.52), kind=kLoop, calls=%fused_computation.6 | loop fusion | flops 524288 | bytes 3145730 | tf_op jit(solution)/shard_map/jit(_where)/select_n | solution.py:119
  93.9 0.1 fusion.22
  94.0 0.3 select_reduce_fusion.1
  94.3 0.2 bitcast_reduce_fusion
  94.5 0.4 fusion
  95.0 0.7 copy.38
  95.6 3.3 %all-to-all-start.2 = ((bf16[2,4,2048]{2,0,1:T(2,128)(2,1)}), bf16[2,4,2048]{2,0,1:T(2,128)(2,1)S(1)}, u32[]{:S(2)}, u32[]{:S(2)}) async-start(bf16[2,4,2048]{2,0,1:T(2,128)(2,1)} %copy.38), calls=%async_computation.3 | async-start | bytes 65536 | tf_op jit(solution)/shard_map/all_to_all | solution.py:127
  98.9 0.8 fusion.5
  99.7 4.8 %all-to-all-done.2 = bf16[2,4,2048]{2,0,1:T(2,128)(2,1)S(1)} async-done(((bf16[2,4,2048]{2,0,1:T(2,128)(2,1)}), bf16[2,4,2048]{2,0,1:T(2,128)(2,1)S(1)}, u32[]{:S(2)}, u32[]{:S(2)}) %all-to-all-start.2) | async-done | bytes 32800 | tf_op jit(solution)/shard_map/all_to_all | solution.py:127
  104.5 0.6 all_to_all.47
  (38 shorter events, 0.2 us)
Async XLA Ops:
  7.2 35.9 %reduce-scatter.2.cloned.1.call-start = ((), (), s32[]{:S(2)}) async-start(), calls=%async_computation.4 | async-start | bytes 1310720 | tf_op jit(solution)/shard_map/reduce_scatter | solution.py:100
  7.2 7.2 %copy-start.5 = (bf16[8,512]{1,0:T(8,128)(2,1)S(1)}, bf16[8,512]{1,0:T(8,128)(2,1)}, u32[]{:S(2)}) copy-start(bf16[8,512]{1,0:T(8,128)(2,1)} %param.20) | copy-start | bytes 24580
  7.2 14.2 %copy-start.9 = (s32[8]{0:T(128)S(1)}, s32[8]{0:T(128)}, u32[]{:S(2)}) copy-start(s32[8]{0:T(128)} %param.22) | copy-start | bytes 100
  7.2 14.3 %copy-start.4 = (s32[24,256]{1,0:T(8,128)S(1)}, s32[24,256]{1,0:T(8,128)}, u32[]{:S(2)}) copy-start(s32[24,256]{1,0:T(8,128)} %param.23) | copy-start | bytes 73732
  7.3 15.4 %copy-start.1 = (bf16[8,7680]{1,0:T(8,128)(2,1)S(1)}, bf16[8,7680]{1,0:T(8,128)(2,1)}, u32[]{:S(2)}) copy-start(bf16[8,7680]{1,0:T(8,128)(2,1)} %param.21) | copy-start | bytes 368644
  7.3 28.6 %copy-start.8 = (s32[2,8]{1,0:T(2,128)S(1)}, s32[2,8]{1,0:T(2,128)}, u32[]{:S(2)}) copy-start(s32[2,8]{1,0:T(2,128)} %param.15) | copy-start | bytes 196
  7.3 43.7 %copy-start.6 = (s32[2,8]{1,0:T(2,128)S(1)}, s32[2,8]{1,0:T(2,128)}, u32[]{:S(2)}) copy-start(s32[2,8]{1,0:T(2,128)} %param.16) | copy-start | bytes 196
  7.3 52.0 %copy-start.2 = (bf16[2,128,2048]{2,1,0:T(8,128)(2,1)S(1)}, bf16[2,128,2048]{2,1,0:T(8,128)(2,1)}, u32[]{:S(2)}) copy-start(bf16[2,128,2048]{2,1,0:T(8,128)(2,1)} %param.17) | copy-start | bytes 3145732
  7.3 53.3 %copy-start.3 = (bf16[8,2048]{1,0:T(8,128)(2,1)S(1)}, bf16[8,2048]{1,0:T(8,128)(2,1)}, u32[]{:S(2)}) copy-start(bf16[8,2048]{1,0:T(8,128)(2,1)} %param.19) | copy-start | bytes 98308
  7.3 54.6 %copy-start.7 = (s32[2]{0:T(128)S(1)}, s32[2]{0:T(128)}, u32[]{:S(2)}) copy-start(s32[2]{0:T(128)} %param.18) | copy-start | bytes 28
  13.5 1.0 copy-start
  15.1 52.0 %all-to-all-start.1 = ((bf16[4,2,512]{2,1,0:T(2,128)(2,1)}), bf16[4,2,512]{2,1,0:T(2,128)(2,1)S(1)}, u32[]{:S(2)}, u32[]{:S(2)}) async-start(bf16[4,2,512]{2,1,0:T(2,128)(2,1)} %all_to_all.41), calls=%async_computation.2 | async-start | bytes 16384 | tf_op jit(solution)/shard_map/all_to_all | solution.py:124
  21.4 66.7 %all-gather.2.cloned.1.call-start = ((), (), s32[]{:S(2)}) async-start(), calls=%async_computation.5 | async-start | bytes 1310720 | tf_op jit(solution)/shard_map/all_gather | solution.py:116
  35.7 26.8 %collective-permute-start.3 = (f32[8]{0:T(128)S(1)}, f32[8]{0:T(128)S(1)}, u32[]{:S(2)}, u32[]{:S(2)}) collective-permute-start(f32[8]{0:T(128)S(1)} %fusion.4), channel_id=1, source_target_pairs={{0,1},{1,0},{2,3},{3,2},{4,5},{5,4},{6,7},{7,6},{8,9},{9,8},{10,11... | collective-permute-start | bytes 104 | tf_op jit(solution)/shard_map/ppermute | solution.py:139
  43.1 9.8 %collective-permute-start = (bf16[64,2048]{1,0:T(8,128)(2,1)}, bf16[64,2048]{1,0:T(8,128)(2,1)S(1)}, u32[]{:S(2)}, u32[]{:S(2)}) collective-permute-start(bf16[64,2048]{1,0:T(8,128)(2,1)} %reduce-scatter.2.cloned.1.call-done), channel_id=1, source_target_pairs={{0,8},{4,12},{8,16},{12,20},{16,24},{20,28},{1,9},{5,13},{9,17},{1... | collective-permute-start | bytes 786440 | tf_op jit(solution)/shard_map/ppermute | solution.py:18
  46.2 12.0 %collective-permute-start.1 = (bf16[64,2048]{1,0:T(8,128)(2,1)}, bf16[64,2048]{1,0:T(8,128)(2,1)S(1)}, u32[]{:S(2)}, u32[]{:S(2)}) collective-permute-start(bf16[64,2048]{1,0:T(8,128)(2,1)} %reduce-scatter.2.cloned.1.call-done), channel_id=1, source_target_pairs={{0,16},{4,20},{8,24},{12,28},{1,17},{5,21},{9,25},{13,29},{2,18},{... | collective-permute-start | bytes 786440 | tf_op jit(solution)/shard_map/ppermute | solution.py:18
  49.6 8.6 %collective-permute-start.2 = (bf16[64,2048]{1,0:T(8,128)(2,1)}, bf16[64,2048]{1,0:T(8,128)(2,1)S(1)}, u32[]{:S(2)}, u32[]{:S(2)}) collective-permute-start(bf16[64,2048]{1,0:T(8,128)(2,1)} %reduce-scatter.2.cloned.1.call-done), channel_id=1, source_target_pairs={{0,24},{4,28},{1,25},{5,29},{2,26},{6,30},{3,27},{7,31}} | collective-permute-start | bytes 786440 | tf_op jit(solution)/shard_map/ppermute | solution.py:18
  62.5 4.5 %collective-permute-start.4 = (f32[8]{0:T(128)S(1)}, f32[8]{0:T(128)S(1)}, u32[]{:S(2)}, u32[]{:S(2)}) collective-permute-start(f32[8]{0:T(128)S(1)} %add.67), channel_id=1, source_target_pairs={{0,2},{1,3},{2,0},{3,1},{4,6},{5,7},{6,4},{7,5},{8,10},{9,11},{10,... | collective-permute-start | bytes 104 | tf_op jit(solution)/shard_map/ppermute | solution.py:139
  67.1 9.3 %all-to-all-start = ((bf16[4,2,2048]{2,1,0:T(2,128)(2,1)}), bf16[4,2,2048]{2,1,0:T(2,128)(2,1)S(1)}, u32[]{:S(2)}, u32[]{:S(2)}) async-start(bf16[4,2,2048]{2,1,0:T(2,128)(2,1)} %all_to_all.38), calls=%async_computation.1 | async-start | bytes 65536 | tf_op jit(solution)/shard_map/all_to_all | solution.py:123
  95.6 8.9 %all-to-all-start.2 = ((bf16[2,4,2048]{2,0,1:T(2,128)(2,1)}), bf16[2,4,2048]{2,0,1:T(2,128)(2,1)S(1)}, u32[]{:S(2)}, u32[]{:S(2)}) async-start(bf16[2,4,2048]{2,0,1:T(2,128)(2,1)} %copy.38), calls=%async_computation.3 | async-start | bytes 65536 | tf_op jit(solution)/shard_map/all_to_all | solution.py:127
Sparse Core Ops, SparseCore 0:
  14.6 28.4 reduce-scatter.1
  59.1 29.0 all-gather.1
